TPU v7x, 256 devices: a whole 4x4x8 slice. The times are simulated.
256 devices in a mesh: dp: 4 (over x), expert: 16 (over z, core), tp: 4 (over y).
Axes of the slice: x: 4, y: 4, z: 8, core: 2. Of those that a mesh axis runs over, the one named last changes fastest.
Arguments:
- hidden: bfloat16 [16, 64, 96, 5632], P('expert', 'dp', None, 'tp'), parts along dimension 1, may hold values from -6 to 6
- down_weight: bfloat16 [16, 5632, 3072], P('expert', 'tp'), may hold values from -0.078125 to 0.078125
- routes: int32 [16384, 4], P(('dp', 'expert')), parts along dimension 0, may hold values from 0 to 15, all different within a row; in each aligned block of 256 rows (0 to 255, 256 to 511, ...) at most 96 rows name the same one
- route_weight: float32 [16384, 4], P(('dp', 'expert')), parts along dimension 0, may hold values from 0.05 to 1
- residual: bfloat16 [16384, 3072], P(('dp', 'expert'), 'tp'), parts along dimension 0, may hold values from -6 to 6
Outputs:
- mixed: bfloat16 [16384, 3072], P(('dp', 'expert'), 'tp'), parts along dimension 0
There are 4 independent parts, one for each index of `dp`. A program takes and returns all parts, laid end to end along the dimension named above; an argument that names none is the same for every part. Nothing has to cross between parts.
Inputs may be any that keep to these rules, and one draw needn't show every extreme that they name: `routes`: each row names 4 different experts. Among the 256 rows of one source group no expert is named by more than 96 rows, a bound that some of them reach.
All inputs are finite; a program needn't handle non-finite values.
Results may differ from a plain program's by a relative error of at most 0.0095.
Values may be sent and summed in bfloat16 or wider, within the bound.
A program may use at most 128 MiB of HBM per device.

v0:
```python
import jax
import jax.numpy as jnp
from jax import lax
from jax.sharding import PartitionSpec as P

EXPERTS = 16


def slot_table(routes):
    expert_ids = jnp.arange(EXPERTS, dtype=jnp.int32)
    matches = (routes[:, :, None] == expert_ids[None, None, :]).astype(jnp.int32)
    onehot = jnp.sum(matches, axis=1)
    before = jnp.cumsum(onehot, axis=0) - onehot
    return jnp.sum(matches * before[:, None, :], axis=2)


def combine(received, routes, route_weight, slot_of):
    capacity = received.shape[1]
    width = received.shape[2]
    flattened = received.reshape(-1, width)
    slot_index = (routes * capacity + slot_of).reshape(-1)
    picked = (
        flattened[slot_index].astype(jnp.float32).reshape(routes.shape[0], routes.shape[1], width)
    )
    share = route_weight / jnp.sum(route_weight, axis=1, keepdims=True)
    return jnp.sum(share[:, :, None] * picked, axis=1)


def on_device(hidden, down_weight, routes, route_weight, residual):
    slot_of = slot_table(routes)
    partial_value = jnp.einsum(
        "lsch,lhd->slcd", hidden, down_weight, preferred_element_type=jnp.float32
    ).astype(jnp.bfloat16)
    received = lax.all_to_all(partial_value, "expert", split_axis=0, concat_axis=1, tiled=True)
    mixed_part = combine(received[0], routes, route_weight, slot_of)
    expert_mix = lax.psum_scatter(
        mixed_part.astype(jnp.bfloat16), "tp", scatter_dimension=1, tiled=True
    ).astype(jnp.float32)
    return (residual.astype(jnp.float32) + expert_mix).astype(jnp.bfloat16)


def solution(mesh):
    return jax.shard_map(
        on_device,
        mesh=mesh,
        in_specs=(
            P("expert", "dp", None, "tp"),
            P("expert", "tp", None),
            P(("dp", "expert"), None),
            P(("dp", "expert"), None),
            P(("dp", "expert"), "tp"),
        ),
        out_specs=P(("dp", "expert"), "tp"),
        check_vma=False,
    )
```

profile of v0, /device:TPU:2, one launch (start us, length us, event | category | flops | bytes accessed | tf_op | source)
XLA Modules:
  0.0 319.9 jit_solution(6353277664045412335)
XLA Ops:
  6.5 20.0 %convert_bitcast_fusion = bf16[16,1,96,3072]{3,2,1,0:T(8,128)(2,1)} fusion(bf16[1,1408,3072]{2,1,0:T(8,128)(2,1)} %param.6, bf16[1,16,96,1408]{3,2,1,0:T(8,128)(2,1)} %param.5), kind=kOutput, calls=%fused_computation.2 | convolution fusion | flops 13292273664 | bytes 22413312 | tf_op jit(solution)/shard_map/lsch,lhd->slcd/dot_general | solution.py:31
  26.5 0.0 copy-start.1
  26.5 0.0 copy-start.2
  26.5 8.8 %all-to-all-start = ((bf16[16,1,96,3072]{3,2,1,0:T(8,128)(2,1)}), bf16[16,1,96,3072]{3,2,1,0:T(8,128)(2,1)}, u32[]{:S(2)}, u32[]{:S(2)}) async-start(bf16[16,1,96,3072]{3,2,1,0:T(8,128)(2,1)} %convert_bitcast_fusion), calls=%async_computation | async-start | bytes 18874368 | tf_op jit(solution)/shard_map/all_to_all | solution.py:34
  35.3 0.0 reduce-scatter.2.cloned.1.call-start
  35.3 0.0 copy-done.1
  35.3 0.6 reduce-window.6
  35.9 0.2 slice_reduce_fusion
  36.2 0.1 fusion.5
  36.3 0.1 copy.25
  36.4 0.1 reshape.65
  36.5 0.0 copy-done.2
  36.6 0.1 copy.21
  36.8 205.1 %all-to-all-done = bf16[16,1,96,3072]{3,2,1,0:T(8,128)(2,1)} async-done(((bf16[16,1,96,3072]{3,2,1,0:T(8,128)(2,1)}), bf16[16,1,96,3072]{3,2,1,0:T(8,128)(2,1)}, u32[]{:S(2)}, u32[]{:S(2)}) %all-to-all-start) | async-done | bytes 9437216 | tf_op jit(solution)/shard_map/all_to_all | solution.py:34
  241.9 17.1 %gather_fusion = bf16[1024,3072]{1,0:T(8,128)(2,1)} fusion(bf16[1536,3072]{1,0:T(8,128)(2,1)} %bitcast.6, s32[1024]{0:T(1024)S(1)} %broadcast_clamp_fusion), kind=kCustom, calls=%fused_computation | custom fusion | bytes 12587008 | tf_op jit(solution)/shard_map/gather | solution.py:23
  259.0 12.2 %reshape.66 = f32[256,4,3072]{2,1,0:T(4,128)} reshape(bf16[1024,3072]{1,0:T(8,128)(2,1)} %gather_fusion) | data formatting | bytes 18874368 | tf_op jit(solution)/shard_map/convert_element_type | solution.py:23
  271.3 0.0 copy-start
  271.3 12.2 %multiply_reduce_fusion = bf16[256,3072]{1,0:T(8,128)(2,1)} fusion(f32[256,4,3072]{2,1,0:T(4,128)} %reshape.66, f32[256,4]{1,0:T(8,128)S(1)} %copy.21), kind=kLoop, calls=%fused_computation.1 | loop fusion | flops 5505024 | bytes 14159872 | tf_op jit(solution)/shard_map/reduce_sum | solution.py:26
  283.5 0.0 reduce-scatter.2.cloned.1.call-update
  283.5 27.7 %reduce-scatter.2.cloned.1.call-done = bf16[256,768]{1,0:T(8,128)(2,1)} async-done(((bf16[256,3072]{1,0:T(8,128)(2,1)}), bf16[256,768]{1,0:T(8,128)(2,1)}) %reduce-scatter.2.cloned.1.call-update) | async-done | bytes 393232 | tf_op jit(solution)/shard_map/reduce_scatter | solution.py:36
  311.2 0.0 copy-done
  311.2 1.8 add_convert_fusion
  (10 shorter events, 0.1 us)
Async XLA Ops:
  26.5 8.8 %copy-start.1 = (s32[256,4]{0,1:T(4,128)S(1)}, s32[256,4]{0,1:T(4,128)}, u32[]{:S(2)}) copy-start(s32[256,4]{0,1:T(4,128)} %param.7) | copy-start | bytes 12292
  26.5 10.1 %copy-start.2 = (f32[256,4]{0,1:T(4,128)S(1)}, f32[256,4]{0,1:T(4,128)}, u32[]{:S(2)}) copy-start(f32[256,4]{0,1:T(4,128)} %param.8) | copy-start | bytes 12292
  26.5 215.4 %all-to-all-start = ((bf16[16,1,96,3072]{3,2,1,0:T(8,128)(2,1)}), bf16[16,1,96,3072]{3,2,1,0:T(8,128)(2,1)}, u32[]{:S(2)}, u32[]{:S(2)}) async-start(bf16[16,1,96,3072]{3,2,1,0:T(8,128)(2,1)} %convert_bitcast_fusion), calls=%async_computation | async-start | bytes 18874368 | tf_op jit(solution)/shard_map/all_to_all | solution.py:34
  35.3 275.9 %reduce-scatter.2.cloned.1.call-start = ((), (), s32[]{:S(2)}) async-start(), calls=%async_computation.2 | async-start | bytes 1966080 | tf_op jit(solution)/shard_map/reduce_scatter | solution.py:36
  271.3 39.9 %copy-start = (bf16[256,768]{1,0:T(8,128)(2,1)S(1)}, bf16[256,768]{1,0:T(8,128)(2,1)}, u32[]{:S(2)}) copy-start(bf16[256,768]{1,0:T(8,128)(2,1)} %param.9) | copy-start | bytes 1179652
Sparse Core Ops, SparseCore 0:
  283.6 27.4 reduce-scatter.1
where the time goes:
time: 320 us
  waiting for transfers between devices  233 us (73%)
  local copies, waits for them, and re-layouts  30 us (9%)
  matrix products  20 us (6%)
  other arithmetic  14.9 us (5%)
  between operations  13.5 us (4%)
  starting transfers between devices  8.79 us (3%)
    all_to_all x1, waiting for transfers between devices, on_device(): lax.all_to_all(partial_value, 'expert', split_axis=0, concat_axis=1, tile...  205 us
    reduce_scatter x1, waiting for transfers between devices, on_device(): lax.psum_scatter(mixed_part.astype(jnp.bfloat16), 'tp', scatter_dimension...  27.7 us
    dot_general x1, matrix products, on_device(): jnp.einsum('lsch,lhd->slcd', hidden, down_weight, preferred_element_type=...  20 us
    gather x1, local copies, waits for them, and re-layouts, combine(): flattened[slot_index].astype(jnp.float32)  17.1 us
    reduce_sum x1, other arithmetic, combine(): return jnp.sum(share[:, :, None] * picked, axis=1)  12.2 us
    convert_element_type x1, local copies, waits for them, and re-layouts, combine(): flattened[slot_index].astype(jnp.float32)  12.2 us
    all_to_all x1, starting transfers between devices, on_device(): lax.all_to_all(partial_value, 'expert', split_axis=0, concat_axis=1, tile...  8.75 us
  transfers between devices with their start and end apart: 2, of which 2 were waited for; matrix products, arithmetic and copies ran while one was open for 0% of the time, Pallas kernels for 0%

commit v1 on v0

--- a/solution.py
+++ b/solution.py
@@ -31,7 +31,11 @@
     partial_value = jnp.einsum(
         "lsch,lhd->slcd", hidden, down_weight, preferred_element_type=jnp.float32
     ).astype(jnp.bfloat16)
-    received = lax.all_to_all(partial_value, "expert", split_axis=0, concat_axis=1, tiled=True)
+    t_next = lax.axis_size("expert")
+    x_new = jnp.split(partial_value, t_next, axis=0)
+    work_now = jnp.stack(x_new)
+    shaped = lax.all_to_all(work_now, axis_name="expert", split_axis=0, concat_axis=0)
+    received = jnp.concatenate(shaped, axis=1)
     mixed_part = combine(received[0], routes, route_weight, slot_of)
     expert_mix = lax.psum_scatter(
         mixed_part.astype(jnp.bfloat16), "tp", scatter_dimension=1, tiled=True

time: 320 us -> 333 us (1.041)
  local copies, waits for them, and re-layouts: 30 us -> 43.8 us
    unnamed x6 -> x21, local copies, waits for them, and re-layouts: 0.01 us -> 13 us
where the time goes in v1:
time: 333 us; the launch traced here: 332 us
  waiting for transfers between devices  233 us (70%)
  local copies, waits for them, and re-layouts  43.8 us (13%)
  matrix products  18.3 us (5%)
  other arithmetic  14.9 us (4%)
  between operations  13.5 us (4%)
  starting transfers between devices  8.97 us (3%)
    all_to_all x1, waiting for transfers between devices, on_device(): lax.all_to_all(work_now, axis_name='expert', split_axis=0, concat_axis=0)  205 us
    reduce_scatter x1, waiting for transfers between devices, on_device(): lax.psum_scatter(mixed_part.astype(jnp.bfloat16), 'tp', scatter_dimension...  27.7 us
    dot_general x1, matrix products, on_device(): jnp.einsum('lsch,lhd->slcd', hidden, down_weight, preferred_element_type=...  18.3 us
    gather x1, local copies, waits for them, and re-layouts, combine(): flattened[slot_index].astype(jnp.float32)  17.1 us
    unnamed x21, local copies, waits for them, and re-layouts  13 us
    reduce_sum x1, other arithmetic, combine(): return jnp.sum(share[:, :, None] * picked, axis=1)  12.2 us
    convert_element_type x1, local copies, waits for them, and re-layouts, combine(): flattened[slot_index].astype(jnp.float32)  12.2 us
    all_to_all x1, starting transfers between devices, on_device(): lax.all_to_all(work_now, axis_name='expert', split_axis=0, concat_axis=0)  8.75 us
  transfers between devices with their start and end apart: 2, of which 2 were waited for; matrix products, arithmetic and copies ran while one was open for 0% of the time, Pallas kernels for 0%

profile of v1, /device:TPU:2, one launch (start us, length us, event | category | flops | bytes accessed | tf_op | source)
XLA Modules:
  0.0 332.1 jit_solution(7942111441979342796)
XLA Ops:
  6.5 18.3 %fusion.2 = bf16[3072,16,96]{0,2,1:T(8,128)(2,1)S(1)} fusion(bf16[1,1408,3072]{2,1,0:T(8,128)(2,1)} %param.6, bf16[1,16,96,1408]{3,2,1,0:T(8,128)(2,1)} %param.5), kind=kOutput, calls=%fused_computation.4 | convolution fusion | flops 13292273664 | bytes 22413312 | tf_op jit(solution)/shard_map/lsch,lhd->slcd/dot_general | solution.py:31
  24.8 0.8 fusion.21
  25.7 0.8 fusion.20
  26.5 0.9 fusion.19
  27.4 0.9 fusion.18
  28.3 0.9 fusion.17
  29.1 0.9 fusion.16
  30.0 0.9 fusion.15
  30.9 0.8 fusion.14
  31.7 0.8 fusion.13
  32.6 0.9 fusion.12
  33.5 0.9 fusion.11
  34.3 0.9 fusion.10
  35.2 0.9 fusion.9
  36.1 0.9 fusion.8
  37.0 0.9 fusion.7
  37.8 0.9 fusion.6
  38.7 0.0 copy-start.1
  38.7 0.0 copy-start.2
  38.7 8.7 %all-to-all-start = ((bf16[16,1,1,96,3072]{4,3,2,1,0:T(8,128)(2,1)}), bf16[16,1,1,96,3072]{4,3,2,1,0:T(8,128)(2,1)}, u32[]{:S(2)}, u32[]{:S(2)}) async-start(bf16[16,1,1,96,3072]{4,3,2,1,0:T(8,128)(2,1)} %fusion.6), calls=%async_computation | async-start | bytes 18874368 | tf_op jit(solution)/shard_map/all_to_all | solution.py:37
  47.5 0.2 reduce-scatter.2.cloned.1.call-start
  47.7 0.0 copy-done.1
  47.7 0.6 reduce-window.6
  48.3 0.2 slice_reduce_fusion
  48.5 0.1 fusion.22
  48.7 0.1 copy.62
  48.8 0.1 reshape.61
  48.9 0.0 copy-done.2
  49.0 0.1 copy.44
  49.2 204.9 %all-to-all-done = bf16[16,1,1,96,3072]{4,3,2,1,0:T(8,128)(2,1)} async-done(((bf16[16,1,1,96,3072]{4,3,2,1,0:T(8,128)(2,1)}), bf16[16,1,1,96,3072]{4,3,2,1,0:T(8,128)(2,1)}, u32[]{:S(2)}, u32[]{:S(2)}) %all-to-all-start) | async-done | bytes 9437216 | tf_op jit(solution)/shard_map/all_to_all | solution.py:37
  254.1 17.1 %gather_fusion = bf16[1024,3072]{1,0:T(8,128)(2,1)} fusion(bf16[1536,3072]{1,0:T(8,128)(2,1)} %bitcast.37, s32[1024]{0:T(1024)S(1)} %broadcast_clamp_fusion), kind=kCustom, calls=%fused_computation | custom fusion | bytes 12587008 | tf_op jit(solution)/shard_map/gather | solution.py:23
  271.2 12.2 %reshape.62 = f32[256,4,3072]{2,1,0:T(4,128)} reshape(bf16[1024,3072]{1,0:T(8,128)(2,1)} %gather_fusion) | data formatting | bytes 18874368 | tf_op jit(solution)/shard_map/convert_element_type | solution.py:23
  283.5 0.0 copy-start
  283.5 12.2 %multiply_reduce_fusion = bf16[256,3072]{1,0:T(8,128)(2,1)} fusion(f32[256,4,3072]{2,1,0:T(4,128)} %reshape.62, f32[256,4]{1,0:T(8,128)S(1)} %copy.44), kind=kLoop, calls=%fused_computation.1 | loop fusion | flops 5505024 | bytes 14159872 | tf_op jit(solution)/shard_map/reduce_sum | solution.py:26
  295.7 0.0 reduce-scatter.2.cloned.1.call-update
  295.7 27.7 %reduce-scatter.2.cloned.1.call-done = bf16[256,768]{1,0:T(8,128)(2,1)} async-done(((bf16[256,3072]{1,0:T(8,128)(2,1)}), bf16[256,768]{1,0:T(8,128)(2,1)}) %reduce-scatter.2.cloned.1.call-update) | async-done | bytes 393232 | tf_op jit(solution)/shard_map/reduce_scatter | solution.py:40
  323.4 0.0 copy-done
  323.4 1.8 add_convert_fusion
  (10 shorter events, 0.1 us)
Async XLA Ops:
  38.7 9.0 %copy-start.1 = (s32[256,4]{0,1:T(4,128)S(1)}, s32[256,4]{0,1:T(4,128)}, u32[]{:S(2)}) copy-start(s32[256,4]{0,1:T(4,128)} %param.7) | copy-start | bytes 12292
  38.7 10.2 %copy-start.2 = (f32[256,4]{0,1:T(4,128)S(1)}, f32[256,4]{0,1:T(4,128)}, u32[]{:S(2)}) copy-start(f32[256,4]{0,1:T(4,128)} %param.8) | copy-start | bytes 12292
  38.7 215.4 %all-to-all-start = ((bf16[16,1,1,96,3072]{4,3,2,1,0:T(8,128)(2,1)}), bf16[16,1,1,96,3072]{4,3,2,1,0:T(8,128)(2,1)}, u32[]{:S(2)}, u32[]{:S(2)}) async-start(bf16[16,1,1,96,3072]{4,3,2,1,0:T(8,128)(2,1)} %fusion.6), calls=%async_computation | async-start | bytes 18874368 | tf_op jit(solution)/shard_map/all_to_all | solution.py:37
  47.5 275.9 %reduce-scatter.2.cloned.1.call-start = ((), (), s32[]{:S(2)}) async-start(), calls=%async_computation.2 | async-start | bytes 1966080 | tf_op jit(solution)/shard_map/reduce_scatter | solution.py:40
  283.5 39.9 %copy-start = (bf16[256,768]{1,0:T(8,128)(2,1)S(1)}, bf16[256,768]{1,0:T(8,128)(2,1)}, u32[]{:S(2)}) copy-start(bf16[256,768]{1,0:T(8,128)(2,1)} %param.9) | copy-start | bytes 1179652
Sparse Core Ops, SparseCore 0:
  295.8 27.4 reduce-scatter.1
